TPU v7x, 32 devices: a whole 2x2x4 slice. The times are simulated.
32 devices in a mesh: grp: 2 (over y), seq: 16 (over z, x, core).
Axes of the slice: x: 2, y: 2, z: 4, core: 2. Of those that a mesh axis runs over, the one named last changes fastest.
Arguments:
- streams: bfloat16 [3, 4096, 4096], P(None, ('grp', 'seq')), parts along dimension 1, may hold values from -12 to 12
- long_filter: bfloat16 [4096, 2048], P('seq'), may hold values from -1 to 1
- gain: bfloat16 [4096], replicated, may hold values from 0.099609375 to 1.8984375
- unembed: bfloat16 [4096, 512], P('seq'), may hold values from -8 to 8
- offsets: int32 [32], P('grp'), parts along dimension 0, may hold values from 0 to 127
- ref_ids: int32 [32], P(('grp', 'seq')), parts along dimension 0, may hold values from 0 to 511
- alt_ids: int32 [32], P(('grp', 'seq')), parts along dimension 0, may hold values from 0 to 511
Outputs:
- mixed: bfloat16 [4096, 4096], P(('grp', 'seq')), parts along dimension 0
- scores: float32 [2, 32], P(None, ('grp', 'seq')), parts along dimension 1
There are 2 independent parts, one for each index of `grp`. A program takes and returns all parts, laid end to end along the dimension named above; an argument that names none is the same for every part. Nothing has to cross between parts.
All inputs are finite; a program needn't handle non-finite values.
Results may differ from a plain program's by a relative error of at most 0.0057.
Values may be sent and summed in bfloat16 or wider, within the bound.
A program may use at most 128 MiB of HBM per device.

v0:
```python
import functools
import math

import jax
import jax.numpy as jnp
import numpy as np
from jax import lax
from jax.experimental import pallas as pl
from jax.experimental.pallas import tpu as pltpu
from jax.sharding import PartitionSpec as P

norm_eps = 1e-06
highest = lax.Precision.HIGHEST
LANES = 128
BLOCK = 256
MESH = pl.DeviceIdType.MESH


def angle_pair(left_count, right_count, period):
    product = (
        jnp.arange(left_count, dtype=jnp.int32)[:, None]
        * jnp.arange(right_count, dtype=jnp.int32)[None, :]
        % period
    )
    theta = product.astype(jnp.float32) * (2.0 * math.pi / period)
    return (jnp.cos(theta), jnp.sin(theta))


def forward_spectrum(signal, outer_cos, outer_sin, twist_cos, twist_sin, inner_cos, inner_sin):
    first_re = jnp.einsum("kn,cnm->ckm", outer_cos, signal, precision=highest)
    first_im = -jnp.einsum("kn,cnm->ckm", outer_sin, signal, precision=highest)
    middle_re = first_re * twist_cos + first_im * twist_sin
    middle_im = first_im * twist_cos - first_re * twist_sin
    spec_re = jnp.einsum("ckn,nm->ckm", middle_re, inner_cos, precision=highest) + jnp.einsum(
        "ckn,nm->ckm", middle_im, inner_sin, precision=highest
    )
    spec_im = jnp.einsum("ckn,nm->ckm", middle_im, inner_cos, precision=highest) - jnp.einsum(
        "ckn,nm->ckm", middle_re, inner_sin, precision=highest
    )
    return (spec_re, spec_im)


def causal_filter(signal_rows, kernel_rows, n_blocks):
    channels, length = signal_rows.shape
    half_rows = length // n_blocks
    outer_len = 2 * half_rows
    period = 2 * length
    outer_cos, outer_sin = angle_pair(outer_len, half_rows, outer_len)
    twist_cos, twist_sin = angle_pair(outer_len, n_blocks, period)
    inner_cos, inner_sin = angle_pair(n_blocks, n_blocks, n_blocks)
    tables = (outer_cos, outer_sin, twist_cos, twist_sin, inner_cos, inner_sin)
    signal_re, signal_im = forward_spectrum(
        signal_rows.astype(jnp.float32).reshape(channels, half_rows, n_blocks), *tables
    )
    kernel_re, kernel_im = forward_spectrum(
        kernel_rows.astype(jnp.float32).reshape(channels, half_rows, n_blocks), *tables
    )
    joint_re = signal_re * kernel_re - signal_im * kernel_im
    joint_im = signal_re * kernel_im + signal_im * kernel_re
    back_re = jnp.einsum("ckn,nm->ckm", joint_re, inner_cos, precision=highest) - jnp.einsum(
        "ckn,nm->ckm", joint_im, inner_sin, precision=highest
    )
    back_im = jnp.einsum("ckn,nm->ckm", joint_im, inner_cos, precision=highest) + jnp.einsum(
        "ckn,nm->ckm", joint_re, inner_sin, precision=highest
    )
    turned_re = back_re * twist_cos - back_im * twist_sin
    turned_im = back_im * twist_cos + back_re * twist_sin
    result = jnp.einsum("kn,ckm->cnm", outer_cos, turned_re, precision=highest) - jnp.einsum(
        "kn,ckm->cnm", outer_sin, turned_im, precision=highest
    )
    return (result / period).reshape(channels, length)


def variant_scores(raw_terms, square_terms, model_width, ref_ids, alt_ids):
    logits = raw_terms * lax.rsqrt(square_terms / model_width + norm_eps)[:, None]
    largest = jnp.max(logits, axis=1)
    log_total = largest + jnp.log(jnp.sum(jnp.exp(logits - largest[:, None]), axis=1))
    vocab_ids = jnp.arange(logits.shape[1], dtype=jnp.int32)
    ref_logit = jnp.sum(jnp.where(vocab_ids[None, :] == ref_ids[:, None], logits, 0.0), axis=1)
    alt_logit = jnp.sum(jnp.where(vocab_ids[None, :] == alt_ids[:, None], logits, 0.0), axis=1)
    return jnp.stack([ref_logit - log_total, alt_logit - ref_logit])


def pick_local(mixed, offsets, my_index, vars_dev):
    stride_rows = mixed.shape[0] // vars_dev
    local_offsets = lax.dynamic_slice_in_dim(offsets, my_index * vars_dev, vars_dev)
    row_index = jnp.arange(vars_dev, dtype=jnp.int32) * stride_rows + local_offsets
    return mixed[row_index]


def plain_shards(streams, long_filter, gain, unembed, offsets, ref_ids, alt_ids):
    n_devices = lax.axis_size("seq")
    my_index = lax.axis_index("seq")
    tok_rows = streams.shape[1]
    model_width = streams.shape[2]
    group_width = model_width // n_devices
    length = tok_rows * n_devices
    vars_dev = ref_ids.shape[0]
    products = (streams[1].astype(jnp.float32) * streams[2].astype(jnp.float32)).astype(
        jnp.bfloat16
    )
    split_view = products.reshape(tok_rows, n_devices, group_width)
    moved_prod = lax.all_to_all(split_view, "seq", split_axis=1, concat_axis=0, tiled=True)
    convolved = causal_filter(moved_prod.reshape(length, group_width).T, long_filter, n_devices)
    filtered_back = convolved.astype(jnp.bfloat16).T.reshape(length, 1, group_width)
    filtered = lax.all_to_all(
        filtered_back, "seq", split_axis=0, concat_axis=1, tiled=True
    ).reshape(tok_rows, model_width)
    mixed = (streams[0].astype(jnp.float32) * filtered.astype(jnp.float32)).astype(jnp.bfloat16)
    picked = pick_local(mixed, offsets, my_index, vars_dev)
    weighted = (picked.astype(jnp.float32) * gain.astype(jnp.float32)[None, :]).astype(jnp.bfloat16)
    square_terms = jnp.sum(jnp.square(picked.astype(jnp.float32)), axis=1)
    raw_terms = jnp.dot(
        weighted,
        lax.all_gather(unembed, "seq", axis=0, tiled=True),
        preferred_element_type=jnp.float32,
    )
    scores = variant_scores(raw_terms, square_terms, model_width, ref_ids, alt_ids)
    return (mixed, scores)


def block_tables(block):
    freq = 2 * np.arange(block)[:, None] + 1
    time = np.arange(block)[None, :]
    period = 4 * block
    theta = (freq * time % period) * (2.0 * np.pi / period)
    forward = np.concatenate([np.cos(theta), -np.sin(theta)], axis=0)
    theta = (freq * (time + block) % period).T * (2.0 * np.pi / period)
    inverse = np.concatenate([np.cos(theta), -np.sin(theta)], axis=1) / block
    split = []
    for table in (forward, inverse):
        high = table.astype(np.float32).astype(jnp.bfloat16)
        low = (table - high.astype(np.float64)).astype(np.float32).astype(jnp.bfloat16)
        split += [high, low]
    return split


def dot32(left, right):
    return jnp.dot(left, right, preferred_element_type=jnp.float32)


def layer_kernel(
    cfg,
    off_hbm, ref_id_ref, alt_id_ref,
    streams_hbm, filter_hbm, gain_hbm, unembed_hbm,
    fwd_hi_hbm, fwd_lo_hbm, inv_hi_hbm, inv_lo_hbm,
    mixed_ref, scores_ref,
    off_ref,
    streams_ref, filter_ref, gain_ref, unembed_ref,
    fwd_hi_ref, fwd_lo_ref, inv_hi_ref, inv_lo_ref,
    prod_out, prod_in, filt_out, filt_in, spec, taps,
    gate_out, gate_in, part_out, part_in, gain_rows,
    ps_sem, pr_sem, fs_sem, fr_sem, gs_sem, gr_sem, qs_sem, qr_sem, in_sem,
):
    n, halves, rows, width, vocab, model_width = cfg
    me = lax.axis_index("seq")
    n_blocks = n * rows // BLOCK
    per_block = BLOCK // rows
    group = halves * width

    barrier = pltpu.get_barrier_semaphore()

    outer = lax.rem(me // (n // 2) + me // (n // 4) + 1, 2)

    def partner(k):
        quarter = n // 4
        turn = lax.rem((k - 1) // quarter + outer, 2)
        far_step = n // 2 + quarter * turn + (quarter - 1 - lax.rem(k - 1, quarter))
        step = jnp.where(k <= n // 2, far_step, n - k)
        bit, out = 1, 0
        while bit < n:
            out = out + bit * lax.rem(me // bit + step // bit, 2)
            bit *= 2
        return out

    def greet(k, carry):
        pl.semaphore_signal(
            barrier, inc=1, device_id={"seq": partner(k)}, device_id_type=MESH
        )
        return carry

    for k in range(1, n):
        greet(k, 0)

    near = me // (n // 2)
    far = 1 - near

    def half_stream(side, sem):
        cols = pl.ds(pl.multiple_of(side * (model_width // 2), LANES), model_width // 2)
        part = (pl.ds(1, 2), slice(None), cols)
        return pltpu.make_async_copy(streams_hbm.at[part], streams_ref.at[part], in_sem.at[sem])

    def load(src, dst, sem):
        return pltpu.make_async_copy(src, dst, in_sem.at[sem])

    far_load = half_stream(far, 0)
    near_load = half_stream(near, 1)
    gate_load = load(streams_hbm.at[0], streams_ref.at[0], 2)
    off_load = load(off_hbm, off_ref, 3)
    tap_loads = [
        load(filter_hbm, filter_ref, 4),
        load(fwd_hi_hbm, fwd_hi_ref, 5),
        load(fwd_lo_hbm, fwd_lo_ref, 6),
    ]
    late_loads = [
        load(inv_hi_hbm, inv_hi_ref, 7),
        load(inv_lo_hbm, inv_lo_ref, 8),
        load(gain_hbm, gain_ref, 9),
        load(unembed_hbm, unembed_ref, 10),
    ]
    for each in [far_load, near_load, off_load, gate_load] + tap_loads + late_loads:
        each.start()

    def lanes(owner, half):
        return pl.ds(pl.multiple_of(owner * group + half * width, LANES), width)

    def product(owner, half):
        cols = lanes(owner, half)
        left = streams_ref[1, :, cols].astype(jnp.float32)
        right = streams_ref[2, :, cols].astype(jnp.float32)
        return (left * right).astype(jnp.bfloat16)

    def copy(src, dst, send_sem, recv_sem, peer):
        return pltpu.make_async_remote_copy(
            src_ref=src, dst_ref=dst, send_sem=send_sem, recv_sem=recv_sem,
            device_id={"seq": peer}, device_id_type=MESH,
        )

    def prod_copy(half, peer, slot):
        return copy(
            prod_out.at[half, peer], prod_in.at[half, slot],
            ps_sem.at[half, peer], pr_sem.at[half, slot], peer,
        )

    def filt_copy(half, peer, slot):
        return copy(
            filt_out.at[half, peer], filt_in.at[half, slot],
            fs_sem.at[half, peer], fr_sem.at[half, slot], peer,
        )

    def gate_copy(peer, slot):
        return copy(gate_out.at[peer], gate_in.at[slot], gs_sem.at[peer], gr_sem.at[slot], peer)

    def part_copy(peer, slot):
        return copy(part_out.at[peer], part_in.at[slot], qs_sem.at[peer], qr_sem.at[slot], peer)

    def over_peers(body):
        def step(k, carry):
            body(partner(k))
            return carry

        lax.fori_loop(1, n, step, 0)

    for half in range(halves):
        def make(peer, half=half):
            prod_out[half, peer] = product(peer, half)

        def pack(first, last, half=half, make=make):
            def step(k, carry):
                make(partner(k))

                @pl.when(k > first)
                def _():
                    prod_copy(half, partner(k - 1), me).start()

                return carry

            lax.fori_loop(first, last, step, 0)
            prod_copy(half, partner(last - 1), me).start()

        if half == 0:
            far_load.wait()

            def make_far(k, carry, make=make):
                make(partner(k))
                return carry

            def send_far(k, carry):
                prod_copy(0, partner(k), me).start()
                return carry

            lax.fori_loop(1, n // 2 + 1, make_far, 0)
            pl.semaphore_wait(barrier, n - 1)
            lax.fori_loop(1, n // 2 + 1, send_far, 0)
            near_load.wait()
        else:
            pack(1, n // 2 + 1)
        pack(n // 2 + 1, n)
        prod_in[half, me] = product(me, half)

    off_load.wait()
    gate_load.wait()
    chosen = lax.broadcasted_iota(jnp.int32, (16, rows), 1) == off_ref[me]
    chosen = jnp.where(chosen, 1.0, 0.0).astype(jnp.bfloat16)

    def make_gate(peer):
        cols = pl.ds(pl.multiple_of(peer * group, LANES), group)
        return dot32(chosen, streams_ref[0, :, cols])[0:1, :]

    def put_gate(peer):
        gate_out[peer] = make_gate(peer)

    over_peers(put_gate)
    over_peers(lambda peer: gate_copy(peer, me).start())
    gate_in[me] = make_gate(me)

    for each in tap_loads:
        each.wait()

    def segment(d, carry):
        taps_d = filter_ref[:, pl.ds(pl.multiple_of(d * BLOCK, LANES), BLOCK)]
        dims = (((1,), (1,)), ((), ()))
        value = lax.dot_general(
            fwd_hi_ref[...], taps_d, dims, preferred_element_type=jnp.float32
        ) + lax.dot_general(fwd_lo_ref[...], taps_d, dims, preferred_element_type=jnp.float32)
        for half in range(halves):
            taps[half, d] = value[:, half * width : (half + 1) * width]
        return carry

    lax.fori_loop(0, n_blocks, segment, 0)
    row_id = lax.broadcasted_iota(jnp.int32, (BLOCK, width), 0)
    sign = jnp.where(row_id % 2 == 0, 1.0, -1.0)
    for half in range(halves):
        def window(step, carry, half=half):
            d = n_blocks - 1 - step
            re = taps[half, d, :BLOCK]
            im = taps[half, d, BLOCK:]
            taps[half, d, :BLOCK] = taps[half, d - 1, :BLOCK] + sign * im
            taps[half, d, BLOCK:] = taps[half, d - 1, BLOCK:] - sign * re
            return carry

        lax.fori_loop(0, n_blocks - 1, window, 0)
        re = taps[half, 0, :BLOCK]
        im = taps[half, 0, BLOCK:]
        taps[half, 0, :BLOCK] = sign * im
        taps[half, 0, BLOCK:] = -sign * re

    def pair_of_blocks(ref, half, first):
        both = [
            ref[half, pl.ds((first + k) * per_block, per_block)].reshape(BLOCK, width)
            for k in range(2)
        ]
        return jnp.concatenate(both, axis=1)

    for each in late_loads:
        each.wait()
    first_pair = far * (n_blocks // 4)

    def pair_at(q):
        return lax.rem(q + first_pair, n_blocks // 2)

    for half in range(halves):
        over_peers(lambda peer, half=half: prod_copy(half, peer, peer).wait_recv())

        def forward(q, carry, half=half):
            x = pair_of_blocks(prod_in, half, 2 * q)
            value = dot32(fwd_hi_ref[...], x) + dot32(fwd_lo_ref[...], x)
            spec[2 * q] = value[:, :width]
            spec[2 * q + 1] = value[:, width:]
            return carry

        lax.fori_loop(0, n_blocks // 2, forward, 0)

        def mix(tile, carry, half=half):
            re_rows = pl.ds(pl.multiple_of(tile * 8, 8), 8)
            im_rows = pl.ds(pl.multiple_of(BLOCK + tile * 8, 8), 8)
            x_re = [spec[i, re_rows] for i in range(n_blocks)]
            x_im = [spec[i, im_rows] for i in range(n_blocks)]
            for i in reversed(range(n_blocks)):
                w_re = None
                for d in range(i + 1):
                    g_re, g_im = taps[half, d, re_rows], taps[half, d, im_rows]
                    a, b = x_re[i - d], x_im[i - d]
                    t_re = a * g_re - b * g_im
                    t_im = a * g_im + b * g_re
                    w_re, w_im = (t_re, t_im) if w_re is None else (w_re + t_re, w_im + t_im)
                spec[i, re_rows] = w_re
                spec[i, im_rows] = w_im
            return carry

        lax.fori_loop(0, BLOCK // 8, mix, 0)

        def send_pair(q, half=half):
            for k in range(2 * per_block):
                peer = pair_at(q) * 2 * per_block + k

                @pl.when(peer != me)
                def _():
                    filt_copy(half, peer, me).start()

        def inverse(q_step, carry, half=half):
            q = pair_at(q_step)
            w = jnp.concatenate([spec[2 * q], spec[2 * q + 1]], axis=1)
            w_hi = w.astype(jnp.bfloat16)
            w_lo = (w - w_hi.astype(jnp.float32)).astype(jnp.bfloat16)
            y = dot32(inv_hi_ref[...], w_hi) + (
                dot32(inv_hi_ref[...], w_lo) + dot32(inv_lo_ref[...], w_hi)
            )
            y = y.astype(jnp.bfloat16)
            for k in range(2):
                part = y[:, k * width : (k + 1) * width].reshape(per_block, rows, width)
                filt_out[half, pl.ds((2 * q + k) * per_block, per_block)] = part

            if half < halves - 1:

                @pl.when(q_step > 0)
                def _():
                    send_pair(q_step - 1)

            return carry

        lax.fori_loop(0, n_blocks // 2, inverse, 0)
        if half < halves - 1:
            send_pair(n_blocks // 2 - 1)

    over_peers(lambda peer: gate_copy(peer, peer).wait_recv())
    variant = lax.broadcasted_iota(jnp.int32, (n, LANES), 0)
    place = jnp.zeros((n, LANES), jnp.int32)
    for j in range(n):
        place = jnp.where(variant == j, off_ref[j], place)
    place = place[:, :1]
    column = lax.broadcasted_iota(jnp.int32, (n, n * rows), 1)
    slot = lax.broadcasted_iota(jnp.int32, (n, n * rows), 0) * rows
    pick = jnp.where(column == slot + place, 1.0, 0.0).astype(jnp.bfloat16)
    picked = [dot32(pick, filt_out[half].reshape(n * rows, width)) for half in range(halves)]
    picked = jnp.concatenate(picked, axis=1)
    gate_rows = gate_in[...].reshape(n, group)
    rows16 = (gate_rows * picked).astype(jnp.bfloat16)
    gain_rows[...] = gain_ref[...].astype(jnp.float32).reshape(1, model_width)
    gain = gain_rows[:, pl.ds(pl.multiple_of(me * group, LANES), group)]
    rows32 = rows16.astype(jnp.float32)
    weighted = (rows32 * gain).astype(jnp.bfloat16)
    raw = dot32(weighted, unembed_ref[...])
    square = jnp.sum(rows32 * rows32, axis=1, keepdims=True)
    part_out[:, :, :vocab] = raw.reshape(n, 1, vocab)
    part_out[:, :, vocab:] = jnp.broadcast_to(square, (n, LANES)).reshape(n, 1, LANES)
    part_in[me] = part_out[me]
    over_peers(lambda peer: part_copy(peer, me).start())
    over_peers(lambda peer: filt_copy(halves - 1, peer, me).start())

    def score():
        over_peers(lambda peer: part_copy(peer, peer).wait_recv())
        total = jnp.sum(part_in[...], axis=0)
        scale = lax.rsqrt(total[:, vocab : vocab + 1] / model_width + norm_eps)
        logits = total[:, :vocab] * scale
        largest = jnp.max(logits, axis=1, keepdims=True)
        log_total = largest + jnp.log(jnp.sum(jnp.exp(logits - largest), axis=1, keepdims=True))
        vocab_ids = lax.broadcasted_iota(jnp.int32, (1, vocab), 1)
        ref_logit = jnp.sum(
            jnp.where(vocab_ids == ref_id_ref[0], logits, 0.0), axis=1, keepdims=True
        )
        alt_logit = jnp.sum(
            jnp.where(vocab_ids == alt_id_ref[0], logits, 0.0), axis=1, keepdims=True
        )
        lane = lax.broadcasted_iota(jnp.int32, (1, 2), 1)
        scores_ref[...] = jnp.where(lane == 0, ref_logit - log_total, alt_logit - ref_logit)

    def finish(owner, half, value):
        cols = lanes(owner, half)
        gate = streams_ref[0, :, cols].astype(jnp.float32)
        mixed_ref[:, cols] = (gate * value.astype(jnp.float32)).astype(jnp.bfloat16)

    for half in range(halves):
        if half == halves - 1:
            score()

        finish(me, half, filt_out[half, me])

        def landed(step, carry, half=half):
            peer = partner(n - step)
            filt_copy(half, peer, peer).wait_recv()
            finish(peer, half, filt_in[half, peer])
            return carry

        lax.fori_loop(1, n, landed, 0)

    def drain(peer):
        for half in range(halves):
            prod_copy(half, peer, me).wait_send()
            filt_copy(half, peer, me).wait_send()
        gate_copy(peer, me).wait_send()
        part_copy(peer, me).wait_send()

    over_peers(drain)


def fused_shards(streams, long_filter, gain, unembed, offsets, ref_ids, alt_ids):
    n = lax.axis_size("seq")
    rows, model_width = streams.shape[1:]
    group = model_width // n
    vocab = unembed.shape[1]
    halves = group // LANES
    width = LANES
    n_blocks = n * rows // BLOCK
    cfg = (n, halves, rows, width, vocab, model_width)
    tables = [jnp.asarray(t) for t in block_tables(BLOCK)]
    vmem = pl.BlockSpec(memory_space=pltpu.VMEM)
    smem = pl.BlockSpec(memory_space=pltpu.SMEM)
    hbm = pl.BlockSpec(memory_space=pltpu.HBM)
    dma = pltpu.SemaphoreType.DMA
    block_buffer = pltpu.VMEM((halves, n, rows, width), jnp.bfloat16)
    operands = [offsets, ref_ids, alt_ids, streams, long_filter, gain, unembed] + tables
    held = [pltpu.SMEM(each.shape, each.dtype) for each in operands[:1]]
    held += [pltpu.VMEM(each.shape, each.dtype) for each in operands[3:]]
    held_out = [pltpu.with_memory_space_constraint(each, pltpu.HBM) for each in operands]
    held_out[1:3] = [ref_ids, alt_ids]
    mixed, scores = pl.pallas_call(
        functools.partial(layer_kernel, cfg),
        out_shape=(
            jax.ShapeDtypeStruct((rows, model_width), jnp.bfloat16),
            jax.ShapeDtypeStruct((1, 2), jnp.float32),
        ),
        in_specs=[hbm] + [smem] * 2 + [hbm] * (len(operands) - 3),
        out_specs=(vmem, vmem),
        scratch_shapes=held
        + [block_buffer] * 4
        + [
            pltpu.VMEM((n_blocks, 2 * BLOCK, width), jnp.float32),
            pltpu.VMEM((halves, n_blocks, 2 * BLOCK, width), jnp.float32),
            pltpu.VMEM((n, 1, group), jnp.float32),
            pltpu.VMEM((n, 1, group), jnp.float32),
            pltpu.VMEM((n, 1, vocab + LANES), jnp.float32),
            pltpu.VMEM((n, 1, vocab + LANES), jnp.float32),
            pltpu.VMEM((1, model_width), jnp.float32),
        ]
        + [dma((halves, n))] * 4
        + [dma((n,))] * 4
        + [dma((11,))],
        compiler_params=pltpu.CompilerParams(
            collective_id=0, has_side_effects=True, vmem_limit_bytes=48 * 2**20
        ),
    )(*held_out)
    return (mixed, scores.T)


def shards(streams, long_filter, gain, unembed, offsets, ref_ids, alt_ids):
    n = lax.axis_size("seq")
    rows, model_width = streams.shape[1:]
    fits = (
        model_width % (n * LANES) == 0
        and BLOCK % rows == 0
        and rows % 16 == 0
        and (n * rows) % (2 * BLOCK) == 0
        and n * rows <= 16 * BLOCK
        and n % 16 == 0
        and n & (n - 1) == 0
        and model_width // n <= 4 * LANES
        and unembed.shape[1] % LANES == 0
        and ref_ids.shape[0] == 1
        and offsets.shape[0] == n
    )
    body = fused_shards if fits else plain_shards
    return body(streams, long_filter, gain, unembed, offsets, ref_ids, alt_ids)


def solution(mesh):
    placed = (
        P(None, ("grp", "seq"), None),
        P("seq", None),
        P(),
        P("seq", None),
        P("grp"),
        P(("grp", "seq")),
        P(("grp", "seq")),
    )
    return jax.shard_map(
        shards,
        mesh=mesh,
        in_specs=placed,
        out_specs=(P(("grp", "seq"), None), P(None, ("grp", "seq"))),
        check_vma=False,
    )
```

profile of v0, /device:TPU:12, one launch (start us, length us, event | category | flops | bytes accessed | tf_op | source)
XLA Modules:
  0.0 58.2 jit_solution(631357668517646385)
XLA Ops:
  1.9 54.8 %shard_map.122 = (bf16[128,4096]{1,0:T(8,128)(2,1)S(1)}, f32[1,2]{1,0:T(1,128)S(1)}) custom-call(s32[16]{0:T(128)} %off_hbm.1, s32[1]{0:T(128)S(6)} %copy.15.ref_id_ref, s32[1]{0:T(128)S(6)} %copy.16.alt_id_ref, bf16[3,128,4096]{2,1,0:T(8,128)(2,1)} %streams_hbm.1, bf16[256,2048]{1,0:T(8,128)(2,1)} %filter_hbm.1, bf16[4096]{0:T(1024)(128)(2,1)} %gain_hbm.1, ...), custom_call_target="tpu_custom_call" | custom-call | tf_op jit(solution)/shard_map/pallas_call | solution.py:507
  56.7 1.0 %copy.17 = bf16[128,4096]{1,0:T(8,128)(2,1)} copy(bf16[128,4096]{1,0:T(8,128)(2,1)S(1)} %get-tuple-element.8) | data formatting | bytes 2097152
  57.7 0.5 copy.18
where the time goes:
time: 58.6 us; the launch traced here: 58.2 us
  Pallas kernels  54.8 us (94%)
  between operations  1.93 us (3%)
  local copies, waits for them, and re-layouts  1.48 us (3%)
    pallas_call x1, Pallas kernels, fused_shards(): pl.pallas_call(functools.partial(layer_kernel, cfg), out_shape=(jax.Shape...  54.8 us
    unnamed x2, local copies, waits for them, and re-layouts  1.48 us

commit v1 on v0

--- a/solution.py
+++ b/solution.py
@@ -13,6 +13,7 @@
 highest = lax.Precision.HIGHEST
 LANES = 128
 BLOCK = 256
+PLANES = 4
 MESH = pl.DeviceIdType.MESH
 
 
@@ -151,6 +152,7 @@
     prod_out, prod_in, filt_out, filt_in, spec, taps,
     gate_out, gate_in, part_out, part_in, gain_rows,
     ps_sem, pr_sem, fs_sem, fr_sem, gs_sem, gr_sem, qs_sem, qr_sem, in_sem,
+    side_in, mids_in, far_side_in,
 ):
     n, halves, rows, width, vocab, model_width = cfg
     me = lax.axis_index("seq")
@@ -160,55 +162,70 @@
 
     barrier = pltpu.get_barrier_semaphore()
 
-    outer = lax.rem(me // (n // 2) + me // (n // 4) + 1, 2)
-
-    def partner(k):
-        quarter = n // 4
-        turn = lax.rem((k - 1) // quarter + outer, 2)
-        far_step = n // 2 + quarter * turn + (quarter - 1 - lax.rem(k - 1, quarter))
-        step = jnp.where(k <= n // 2, far_step, n - k)
+    team = n // PLANES
+    plane = me // team
+    spot = lax.rem(me, team)
+    is_mid = lax.rem((plane + 1) // 2, 2)
+    is_outer = 1 - is_mid
+
+    def flip(value, step, size):
         bit, out = 1, 0
-        while bit < n:
-            out = out + bit * lax.rem(me // bit + step // bit, 2)
+        while bit < size:
+            out = out + bit * lax.rem(value // bit + step // bit, 2)
             bit *= 2
         return out
 
-    def greet(k, carry):
-        pl.semaphore_signal(
-            barrier, inc=1, device_id={"seq": partner(k)}, device_id_type=MESH
-        )
-        return carry
-
-    for k in range(1, n):
-        greet(k, 0)
-
-    near = me // (n // 2)
-    far = 1 - near
-
-    def half_stream(side, sem):
-        cols = pl.ds(pl.multiple_of(side * (model_width // 2), LANES), model_width // 2)
-        part = (pl.ds(1, 2), slice(None), cols)
-        return pltpu.make_async_copy(streams_hbm.at[part], streams_ref.at[part], in_sem.at[sem])
+    def peer_at(plane_step, spot_step):
+        return flip(plane, plane_step, PLANES) * team + flip(spot, spot_step, team)
+
+    def far_step(k):
+        return 3 - k + jnp.where(k < 2, is_mid * (2 * k - 1), 0)
+
+    def partner(k):
+        return peer_at(far_step((k - 1) // team), team - 1 - lax.rem(k - 1, team))
+
+    def signal(sem, peer):
+        pl.semaphore_signal(sem, inc=1, device_id={"seq": peer}, device_id_type=MESH)
+
+    def greet(plane_step, first):
+        for k in range(first, team):
+            signal(barrier, peer_at(plane_step, k))
+
+    @pl.when(is_mid == 1)
+    def _():
+        greet(3, 0)
+        greet(1, 0)
+
+    greet(0, 1)
+
+    def early_step(k):
+        mid_steps, outer_steps = (3, 0, 1, 2), (1, 0, 2, 3)
+        return outer_steps[k] + (mid_steps[k] - outer_steps[k]) * is_mid
+
+    def plane_stream(k):
+        share = model_width // PLANES
+        first = pl.multiple_of(flip(plane, early_step(k), PLANES) * share, LANES)
+        part = (pl.ds(1, 2), slice(None), pl.ds(first, share))
+        return pltpu.make_async_copy(streams_hbm.at[part], streams_ref.at[part], in_sem.at[k])
 
     def load(src, dst, sem):
         return pltpu.make_async_copy(src, dst, in_sem.at[sem])
 
-    far_load = half_stream(far, 0)
-    near_load = half_stream(near, 1)
-    gate_load = load(streams_hbm.at[0], streams_ref.at[0], 2)
-    off_load = load(off_hbm, off_ref, 3)
+    plane_loads = [plane_stream(k) for k in range(PLANES)]
+    gate_load = load(streams_hbm.at[0], streams_ref.at[0], 4)
+    off_load = load(off_hbm, off_ref, 5)
     tap_loads = [
-        load(filter_hbm, filter_ref, 4),
-        load(fwd_hi_hbm, fwd_hi_ref, 5),
-        load(fwd_lo_hbm, fwd_lo_ref, 6),
+        load(filter_hbm, filter_ref, 6),
+        load(fwd_hi_hbm, fwd_hi_ref, 7),
+        load(fwd_lo_hbm, fwd_lo_ref, 8),
     ]
     late_loads = [
-        load(inv_hi_hbm, inv_hi_ref, 7),
-        load(inv_lo_hbm, inv_lo_ref, 8),
-        load(gain_hbm, gain_ref, 9),
-        load(unembed_hbm, unembed_ref, 10),
+        load(inv_hi_hbm, inv_hi_ref, 9),
+        load(inv_lo_hbm, inv_lo_ref, 10),
+        load(gain_hbm, gain_ref, 11),
+        load(unembed_hbm, unembed_ref, 12),
     ]
-    for each in [far_load, near_load, off_load, gate_load] + tap_loads + late_loads:
+    for each in plane_loads + [off_load, gate_load] + tap_loads + late_loads:
         each.start()
 
     def lanes(owner, half):
@@ -251,42 +268,73 @@
 
         lax.fori_loop(1, n, step, 0)
 
-    for half in range(halves):
-        def make(peer, half=half):
-            prod_out[half, peer] = product(peer, half)
-
-        def pack(first, last, half=half, make=make):
-            def step(k, carry):
-                make(partner(k))
-
-                @pl.when(k > first)
-                def _():
-                    prod_copy(half, partner(k - 1), me).start()
-
-                return carry
-
-            lax.fori_loop(first, last, step, 0)
-            prod_copy(half, partner(last - 1), me).start()
-
-        if half == 0:
-            far_load.wait()
-
-            def make_far(k, carry, make=make):
-                make(partner(k))
-                return carry
-
-            def send_far(k, carry):
-                prod_copy(0, partner(k), me).start()
-                return carry
-
-            lax.fori_loop(1, n // 2 + 1, make_far, 0)
-            pl.semaphore_wait(barrier, n - 1)
-            lax.fori_loop(1, n // 2 + 1, send_far, 0)
-            near_load.wait()
-        else:
-            pack(1, n // 2 + 1)
-        pack(n // 2 + 1, n)
-        prod_in[half, me] = product(me, half)
+    def make_plane(half, plane_step):
+        def step(k, carry):
+            owner = peer_at(plane_step, k)
+            prod_out[half, owner] = product(owner, half)
+            return carry
+
+        lax.fori_loop(0, team, step, 0)
+
+    def send_plane(half, plane_step, first):
+        def step(k, carry):
+            prod_copy(half, peer_at(plane_step, k), me).start()
+            return carry
+
+        lax.fori_loop(first, team, step, 0)
+
+    @pl.when(is_outer == 1)
+    def _():
+        pl.semaphore_wait(barrier, 2 * team - 1)
+        for k in range(team):
+            signal(side_in, peer_at(1, k))
+
+    plane_loads[0].wait()
+    make_plane(0, early_step(0))
+
+    @pl.when(is_mid == 1)
+    def _():
+        pl.semaphore_wait(barrier, 2 * team - 1)
+
+    send_plane(0, early_step(0), 0)
+    plane_loads[1].wait()
+    make_plane(0, 0)
+    prod_in[0, me] = prod_out[0, me]
+    send_plane(0, 0, 1)
+
+    @pl.when(is_mid == 1)
+    def _():
+        pl.semaphore_wait(side_in, team)
+        signal(far_side_in, peer_at(3, 0))
+        signal(mids_in, peer_at(1, 0))
+
+    plane_loads[2].wait()
+    make_plane(0, early_step(2))
+
+    @pl.when(is_outer == 1)
+    def _():
+        pl.semaphore_wait(mids_in, 1)
+
+    send_plane(0, early_step(2), 0)
+    plane_loads[3].wait()
+    make_plane(0, early_step(3))
+
+    pl.semaphore_wait(far_side_in, 1)
+
+    @pl.when(is_mid == 1)
+    def _():
+        signal(far_side_in, peer_at(1, 0))
+
+    send_plane(0, early_step(3), 0)
+    for half in range(1, halves):
+        for k in range(PLANES):
+            make_plane(half, k)
+        prod_in[half, me] = prod_out[half, me]
+
+    def send_rest():
+        for half in range(1, halves):
+            over_peers(lambda peer, half=half: prod_copy(half, peer, me).start())
+        over_peers(lambda peer: gate_copy(peer, me).start())
 
     off_load.wait()
     gate_load.wait()
@@ -301,8 +349,8 @@
         gate_out[peer] = make_gate(peer)
 
     over_peers(put_gate)
-    over_peers(lambda peer: gate_copy(peer, me).start())
     gate_in[me] = make_gate(me)
+    pl.when(is_outer == 1)(send_rest)
 
     for each in tap_loads:
         each.wait()
@@ -344,13 +392,14 @@
 
     for each in late_loads:
         each.wait()
-    first_pair = far * (n_blocks // 4)
 
     def pair_at(q):
-        return lax.rem(q + first_pair, n_blocks // 2)
+        return flip(plane, far_step(q), PLANES)
 
     for half in range(halves):
         over_peers(lambda peer, half=half: prod_copy(half, peer, peer).wait_recv())
+        if half == 0:
+            pl.when(is_mid == 1)(send_rest)
 
         def forward(q, carry, half=half):
             x = pair_of_blocks(prod_in, half, 2 * q)
@@ -381,8 +430,8 @@
         lax.fori_loop(0, BLOCK // 8, mix, 0)
 
         def send_pair(q, half=half):
-            for k in range(2 * per_block):
-                peer = pair_at(q) * 2 * per_block + k
+            for k in reversed(range(team)):
+                peer = pair_at(q) * team + flip(spot, k, team)
 
                 @pl.when(peer != me)
                 def _():
@@ -525,7 +574,8 @@
         ]
         + [dma((halves, n))] * 4
         + [dma((n,))] * 4
-        + [dma((11,))],
+        + [dma((13,))]
+        + [pltpu.SemaphoreType.REGULAR] * 3,
         compiler_params=pltpu.CompilerParams(
             collective_id=0, has_side_effects=True, vmem_limit_bytes=48 * 2**20
         ),
@@ -540,8 +590,7 @@
         model_width % (n * LANES) == 0
         and BLOCK % rows == 0
         and rows % 16 == 0
-        and (n * rows) % (2 * BLOCK) == 0
-        and n * rows <= 16 * BLOCK
+        and n * rows == 2 * PLANES * BLOCK
         and n % 16 == 0
         and n & (n - 1) == 0
         and model_width // n <= 4 * LANES

time: 58.6 us -> 57 us (0.973)
  Pallas kernels: 54.8 us -> 53.2 us
    pallas_call x1, Pallas kernels: 54.8 us -> 53.2 us  [fused_shards(): pl.pallas_call(functools.partial(layer_kernel, cfg), out_shape=(jax.Shape...]
where the time goes in v1:
time: 57 us; the launch traced here: 56.6 us
  Pallas kernels  53.2 us (93%)
  between operations  1.93 us (3%)
  local copies, waits for them, and re-layouts  1.48 us (3%)
    pallas_call x1, Pallas kernels, fused_shards(): pl.pallas_call(functools.partial(layer_kernel, cfg), out_shape=(jax.Shape...  53.2 us
    unnamed x2, local copies, waits for them, and re-layouts  1.48 us

profile of v1, /device:TPU:12, one launch (start us, length us, event | category | flops | bytes accessed | tf_op | source)
XLA Modules:
  0.0 56.6 jit_solution(1512951071030488850)
XLA Ops:
  1.9 53.2 %shard_map.122 = (bf16[128,4096]{1,0:T(8,128)(2,1)S(1)}, f32[1,2]{1,0:T(1,128)S(1)}) custom-call(s32[16]{0:T(128)} %off_hbm.1, s32[1]{0:T(128)S(6)} %copy.15.ref_id_ref, s32[1]{0:T(128)S(6)} %copy.16.alt_id_ref, bf16[3,128,4096]{2,1,0:T(8,128)(2,1)} %streams_hbm.1, bf16[256,2048]{1,0:T(8,128)(2,1)} %filter_hbm.1, bf16[4096]{0:T(1024)(128)(2,1)} %gain_hbm.1, ...), custom_call_target="tpu_custom_call" | custom-call | tf_op jit(solution)/shard_map/pallas_call | solution.py:556
  55.1 1.0 %copy.17 = bf16[128,4096]{1,0:T(8,128)(2,1)} copy(bf16[128,4096]{1,0:T(8,128)(2,1)S(1)} %get-tuple-element.8) | data formatting | bytes 2097152
  56.1 0.5 copy.18

commit v2 on v1

--- a/solution.py
+++ b/solution.py
@@ -14,6 +14,8 @@
 LANES = 128
 BLOCK = 256
 PLANES = 4
+STORES = 4
+GATE = jnp.bfloat16
 MESH = pl.DeviceIdType.MESH
 
 
@@ -150,8 +152,8 @@
     streams_ref, filter_ref, gain_ref, unembed_ref,
     fwd_hi_ref, fwd_lo_ref, inv_hi_ref, inv_lo_ref,
     prod_out, prod_in, filt_out, filt_in, spec, taps,
-    gate_out, gate_in, part_out, part_in, gain_rows,
-    ps_sem, pr_sem, fs_sem, fr_sem, gs_sem, gr_sem, qs_sem, qr_sem, in_sem,
+    gate_out, gate_in, part_out, part_in, line_out, line_in, gain_rows,
+    ps_sem, pr_sem, fs_sem, fr_sem, gs_sem, gr_sem, qs_sem, qr_sem, ls_sem, lr_sem, in_sem,
     side_in, mids_in, far_side_in,
 ):
     n, halves, rows, width, vocab, model_width = cfg
@@ -183,6 +185,9 @@
 
     def partner(k):
         return peer_at(far_step((k - 1) // team), team - 1 - lax.rem(k - 1, team))
+
+    def rank(owner):
+        return lax.rem(owner, team) * PLANES + owner // team
 
     def signal(sem, peer):
         pl.semaphore_signal(sem, inc=1, device_id={"seq": peer}, device_id_type=MESH)
@@ -256,10 +261,23 @@
         )
 
     def gate_copy(peer, slot):
-        return copy(gate_out.at[peer], gate_in.at[slot], gs_sem.at[peer], gr_sem.at[slot], peer)
-
-    def part_copy(peer, slot):
-        return copy(part_out.at[peer], part_in.at[slot], qs_sem.at[peer], qr_sem.at[slot], peer)
+        return copy(
+            gate_out.at[peer], gate_in.at[rank(slot)], gs_sem.at[peer], gr_sem.at[slot], peer
+        )
+
+    def part_copy(step, slot):
+        mate = flip(spot, step, team)
+        return copy(
+            part_out.at[mate], part_in.at[slot], qs_sem.at[mate], qr_sem.at[slot],
+            peer_at(0, step),
+        )
+
+    def line_copy(step, slot):
+        other = flip(plane, step, PLANES)
+        return copy(
+            line_out.at[other], line_in.at[slot], ls_sem.at[other], lr_sem.at[slot],
+            peer_at(step, 0),
+        )
 
     def over_peers(body):
         def step(k, carry):
@@ -343,13 +361,13 @@
 
     def make_gate(peer):
         cols = pl.ds(pl.multiple_of(peer * group, LANES), group)
-        return dot32(chosen, streams_ref[0, :, cols])[0:1, :]
+        return dot32(chosen, streams_ref[0, :, cols])[0:1, :].astype(GATE)
 
     def put_gate(peer):
         gate_out[peer] = make_gate(peer)
 
     over_peers(put_gate)
-    gate_in[me] = make_gate(me)
+    gate_in[rank(me)] = make_gate(me)
     pl.when(is_outer == 1)(send_rest)
 
     for each in tap_loads:
@@ -395,6 +413,14 @@
 
     def pair_at(q):
         return flip(plane, far_step(q), PLANES)
+
+    def send_pair(q, half):
+        for k in reversed(range(team)):
+            peer = pair_at(q) * team + flip(spot, k, team)
+
+            @pl.when(peer != me)
+            def _():
+                filt_copy(half, peer, me).start()
 
     for half in range(halves):
         over_peers(lambda peer, half=half: prod_copy(half, peer, peer).wait_recv())
@@ -429,14 +455,6 @@
 
         lax.fori_loop(0, BLOCK // 8, mix, 0)
 
-        def send_pair(q, half=half):
-            for k in reversed(range(team)):
-                peer = pair_at(q) * team + flip(spot, k, team)
-
-                @pl.when(peer != me)
-                def _():
-                    filt_copy(half, peer, me).start()
-
         def inverse(q_step, carry, half=half):
             q = pair_at(q_step)
             w = jnp.concatenate([spec[2 * q], spec[2 * q + 1]], axis=1)
@@ -450,30 +468,32 @@
                 part = y[:, k * width : (k + 1) * width].reshape(per_block, rows, width)
                 filt_out[half, pl.ds((2 * q + k) * per_block, per_block)] = part
 
-            if half < halves - 1:
-
-                @pl.when(q_step > 0)
-                def _():
-                    send_pair(q_step - 1)
+            @pl.when(q_step > 0 if half < halves - 1 else q_step == 1)
+            def _():
+                send_pair(q_step - 1, half)
 
             return carry
 
         lax.fori_loop(0, n_blocks // 2, inverse, 0)
         if half < halves - 1:
-            send_pair(n_blocks // 2 - 1)
+            send_pair(n_blocks // 2 - 1, half)
+
+    def finish(owner, half, value):
+        cols = lanes(owner, half)
+        gate = streams_ref[0, :, cols].astype(jnp.float32)
+        mixed_ref[:, cols] = (gate * value.astype(jnp.float32)).astype(jnp.bfloat16)
 
     over_peers(lambda peer: gate_copy(peer, peer).wait_recv())
     variant = lax.broadcasted_iota(jnp.int32, (n, LANES), 0)
     place = jnp.zeros((n, LANES), jnp.int32)
     for j in range(n):
-        place = jnp.where(variant == j, off_ref[j], place)
-    place = place[:, :1]
+        j_rank = j % team * PLANES + j // team
+        place = jnp.where(variant == j_rank, off_ref[j] + j * rows, place)
     column = lax.broadcasted_iota(jnp.int32, (n, n * rows), 1)
-    slot = lax.broadcasted_iota(jnp.int32, (n, n * rows), 0) * rows
-    pick = jnp.where(column == slot + place, 1.0, 0.0).astype(jnp.bfloat16)
+    pick = jnp.where(column == place[:, :1], 1.0, 0.0).astype(jnp.bfloat16)
     picked = [dot32(pick, filt_out[half].reshape(n * rows, width)) for half in range(halves)]
     picked = jnp.concatenate(picked, axis=1)
-    gate_rows = gate_in[...].reshape(n, group)
+    gate_rows = gate_in[...].astype(jnp.float32).reshape(n, group)
     rows16 = (gate_rows * picked).astype(jnp.bfloat16)
     gain_rows[...] = gain_ref[...].astype(jnp.float32).reshape(1, model_width)
     gain = gain_rows[:, pl.ds(pl.multiple_of(me * group, LANES), group)]
@@ -481,15 +501,26 @@
     weighted = (rows32 * gain).astype(jnp.bfloat16)
     raw = dot32(weighted, unembed_ref[...])
     square = jnp.sum(rows32 * rows32, axis=1, keepdims=True)
-    part_out[:, :, :vocab] = raw.reshape(n, 1, vocab)
-    part_out[:, :, vocab:] = jnp.broadcast_to(square, (n, LANES)).reshape(n, 1, LANES)
-    part_in[me] = part_out[me]
-    over_peers(lambda peer: part_copy(peer, me).start())
-    over_peers(lambda peer: filt_copy(halves - 1, peer, me).start())
+    part_out[:, :, :vocab] = raw.reshape(team, PLANES, vocab)
+    part_out[:, :, vocab:] = jnp.broadcast_to(square, (n, LANES)).reshape(team, PLANES, LANES)
+    part_in[spot] = part_out[spot]
+    for k in range(1, team):
+        part_copy(k, spot).start()
+    for half in range(halves):
+        finish(me, half, filt_out[half, me])
+    for k in range(1, team):
+        part_copy(k, flip(spot, k, team)).wait_recv()
+    line_out[...] = jnp.sum(part_in[...], axis=0).reshape(PLANES, 1, vocab + LANES)
+    line_in[plane] = line_out[plane]
+    for k in reversed(range(1, PLANES)):
+        line_copy(k, plane).start()
+    for k in range(1, n_blocks // 2):
+        send_pair(k, halves - 1)
 
     def score():
-        over_peers(lambda peer: part_copy(peer, peer).wait_recv())
-        total = jnp.sum(part_in[...], axis=0)
+        for k in range(1, PLANES):
+            line_copy(k, flip(plane, k, PLANES)).wait_recv()
+        total = jnp.sum(line_in[...], axis=0)
         scale = lax.rsqrt(total[:, vocab : vocab + 1] / model_width + norm_eps)
         logits = total[:, :vocab] * scale
         largest = jnp.max(logits, axis=1, keepdims=True)
@@ -504,16 +535,9 @@
         lane = lax.broadcasted_iota(jnp.int32, (1, 2), 1)
         scores_ref[...] = jnp.where(lane == 0, ref_logit - log_total, alt_logit - ref_logit)
 
-    def finish(owner, half, value):
-        cols = lanes(owner, half)
-        gate = streams_ref[0, :, cols].astype(jnp.float32)
-        mixed_ref[:, cols] = (gate * value.astype(jnp.float32)).astype(jnp.bfloat16)
-
     for half in range(halves):
         if half == halves - 1:
             score()
-
-        finish(me, half, filt_out[half, me])
 
         def landed(step, carry, half=half):
             peer = partner(n - step)
@@ -528,15 +552,31 @@
             prod_copy(half, peer, me).wait_send()
             filt_copy(half, peer, me).wait_send()
         gate_copy(peer, me).wait_send()
-        part_copy(peer, me).wait_send()
 
     over_peers(drain)
+    for k in range(1, team):
+        part_copy(k, spot).wait_send()
+    for k in range(1, PLANES):
+        line_copy(k, plane).wait_send()
+
+
+def store_kernel(mixed_ref, scores_ref, mixed_hbm, scores_hbm, sem):
+    share = mixed_ref.shape[0] // STORES
+    moves = [pltpu.make_async_copy(scores_ref, scores_hbm, sem.at[STORES])]
+    for k in range(STORES):
+        part = pl.ds(k * share, share)
+        moves.append(pltpu.make_async_copy(mixed_ref.at[part], mixed_hbm.at[part], sem.at[k]))
+    for move in moves:
+        move.start()
+    for move in moves:
+        move.wait()
 
 
 def fused_shards(streams, long_filter, gain, unembed, offsets, ref_ids, alt_ids):
     n = lax.axis_size("seq")
     rows, model_width = streams.shape[1:]
     group = model_width // n
+    team = n // PLANES
     vocab = unembed.shape[1]
     halves = group // LANES
     width = LANES
@@ -566,20 +606,37 @@
         + [
             pltpu.VMEM((n_blocks, 2 * BLOCK, width), jnp.float32),
             pltpu.VMEM((halves, n_blocks, 2 * BLOCK, width), jnp.float32),
-            pltpu.VMEM((n, 1, group), jnp.float32),
-            pltpu.VMEM((n, 1, group), jnp.float32),
-            pltpu.VMEM((n, 1, vocab + LANES), jnp.float32),
-            pltpu.VMEM((n, 1, vocab + LANES), jnp.float32),
+            pltpu.VMEM((n, 1, group), GATE),
+            pltpu.VMEM((n, 1, group), GATE),
+            pltpu.VMEM((team, PLANES, vocab + LANES), jnp.float32),
+            pltpu.VMEM((team, PLANES, vocab + LANES), jnp.float32),
+            pltpu.VMEM((PLANES, 1, vocab + LANES), jnp.float32),
+            pltpu.VMEM((PLANES, 1, vocab + LANES), jnp.float32),
             pltpu.VMEM((1, model_width), jnp.float32),
         ]
         + [dma((halves, n))] * 4
-        + [dma((n,))] * 4
+        + [dma((n,))] * 2
+        + [dma((team,))] * 2
+        + [dma((PLANES,))] * 2
         + [dma((13,))]
         + [pltpu.SemaphoreType.REGULAR] * 3,
         compiler_params=pltpu.CompilerParams(
             collective_id=0, has_side_effects=True, vmem_limit_bytes=48 * 2**20
         ),
     )(*held_out)
+    mixed, scores = pl.pallas_call(
+        store_kernel,
+        out_shape=(
+            jax.ShapeDtypeStruct(mixed.shape, mixed.dtype),
+            jax.ShapeDtypeStruct(scores.shape, scores.dtype),
+        ),
+        in_specs=[vmem, vmem],
+        out_specs=(hbm, hbm),
+        scratch_shapes=[dma((STORES + 1,))],
+    )(
+        pltpu.with_memory_space_constraint(mixed, pltpu.VMEM),
+        pltpu.with_memory_space_constraint(scores, pltpu.VMEM),
+    )
     return (mixed, scores.T)
 
 

time: 57 us -> 56.3 us (0.988); the launches traced: 56.6 us -> 55.3 us
  local copies, waits for them, and re-layouts: 1.48 us -> 0 us
    unnamed x2 -> x0, local copies, waits for them, and re-layouts: 1.48 us -> none
    pallas_call x0 -> x1, Pallas kernels: none -> 1.01 us  [fused_shards(): pl.pallas_call(store_kernel, out_shape=(jax.ShapeDtypeStruct(mixed.shape,...]
    pallas_call x1, Pallas kernels: 53.2 us -> 52.4 us  [fused_shards(): pl.pallas_call(functools.partial(layer_kernel, cfg), out_shape=(jax.Shape...]
where the time goes in v2:
time: 56.3 us; the launch traced here: 55.3 us
  Pallas kernels  53.4 us (95%)
  between operations  1.93 us (3%)
    pallas_call x1, Pallas kernels, fused_shards(): pl.pallas_call(functools.partial(layer_kernel, cfg), out_shape=(jax.Shape...  52.4 us

profile of v2, /device:TPU:12, one launch (start us, length us, event | category | flops | bytes accessed | tf_op | source)
XLA Modules:
  0.0 55.3 jit_solution(16581436956455364749)
XLA Ops:
  1.9 52.4 %shard_map.122 = (bf16[128,4096]{1,0:T(8,128)(2,1)S(1)}, f32[1,2]{1,0:T(1,128)S(1)}) custom-call(s32[16]{0:T(128)} %off_hbm.1, s32[1]{0:T(128)S(6)} %copy.13.ref_id_ref, s32[1]{0:T(128)S(6)} %copy.14.alt_id_ref, bf16[3,128,4096]{2,1,0:T(8,128)(2,1)} %streams_hbm.1, bf16[256,2048]{1,0:T(8,128)(2,1)} %filter_hbm.1, bf16[4096]{0:T(1024)(128)(2,1)} %gain_hbm.1, ...), custom_call_target="tpu_custom_call" | custom-call | tf_op jit(solution)/shard_map/pallas_call | solution.py:596
  54.3 1.0 %shard_map.123 = (bf16[128,4096]{1,0:T(8,128)(2,1)}, f32[1,2]{1,0:T(1,128)}) custom-call(bf16[128,4096]{1,0:T(8,128)(2,1)S(1)} %get-tuple-element.6.mixed_ref, f32[1,2]{1,0:T(1,128)S(1)} %get-tuple-element.7.scores_ref), custom_call_target="tpu_custom_call" | custom-call | tf_op jit(solution)/shard_map/pallas_call | solution.py:627

commit v3 on v2

--- a/solution.py
+++ b/solution.py
@@ -152,8 +152,8 @@
     streams_ref, filter_ref, gain_ref, unembed_ref,
     fwd_hi_ref, fwd_lo_ref, inv_hi_ref, inv_lo_ref,
     prod_out, prod_in, filt_out, filt_in, spec, taps,
-    gate_out, gate_in, part_out, part_in, line_out, line_in, gain_rows,
-    ps_sem, pr_sem, fs_sem, fr_sem, gs_sem, gr_sem, qs_sem, qr_sem, ls_sem, lr_sem, in_sem,
+    gate_out, gate_mid, gate_in, part_out, part_in, line_out, line_in, gain_rows,
+    ps_sem, pr_sem, fs_sem, fr_sem, gs_sem, gr_sem, hs_sem, hr_sem, qs_sem, qr_sem, ls_sem, lr_sem, in_sem,
     side_in, mids_in, far_side_in,
 ):
     n, halves, rows, width, vocab, model_width = cfg
@@ -185,9 +185,6 @@
 
     def partner(k):
         return peer_at(far_step((k - 1) // team), team - 1 - lax.rem(k - 1, team))
-
-    def rank(owner):
-        return lax.rem(owner, team) * PLANES + owner // team
 
     def signal(sem, peer):
         pl.semaphore_signal(sem, inc=1, device_id={"seq": peer}, device_id_type=MESH)
@@ -260,9 +257,18 @@
             fs_sem.at[half, peer], fr_sem.at[half, slot], peer,
         )
 
-    def gate_copy(peer, slot):
+    def gate_line(step, slot):
+        other = flip(plane, step, PLANES)
         return copy(
-            gate_out.at[peer], gate_in.at[rank(slot)], gs_sem.at[peer], gr_sem.at[slot], peer
+            gate_out.at[pl.ds(other * team, team)], gate_mid.at[slot],
+            gs_sem.at[other], gr_sem.at[slot], peer_at(step, 0),
+        )
+
+    def gate_copy(step, slot):
+        mate = flip(spot, step, team)
+        return copy(
+            gate_mid.at[:, mate], gate_in.at[slot], hs_sem.at[mate], hr_sem.at[slot],
+            peer_at(0, step),
         )
 
     def part_copy(step, slot):
@@ -352,7 +358,6 @@
     def send_rest():
         for half in range(1, halves):
             over_peers(lambda peer, half=half: prod_copy(half, peer, me).start())
-        over_peers(lambda peer: gate_copy(peer, me).start())
 
     off_load.wait()
     gate_load.wait()
@@ -367,8 +372,11 @@
         gate_out[peer] = make_gate(peer)
 
     over_peers(put_gate)
-    gate_in[rank(me)] = make_gate(me)
-    pl.when(is_outer == 1)(send_rest)
+    put_gate(me)
+    gate_mid[plane] = gate_out[pl.ds(plane * team, team)]
+    for k in reversed(range(1, PLANES)):
+        gate_line(k, plane).start()
+    pl.when(is_mid == 1)(send_rest)
 
     for each in tap_loads:
         each.wait()
@@ -425,7 +433,7 @@
     for half in range(halves):
         over_peers(lambda peer, half=half: prod_copy(half, peer, peer).wait_recv())
         if half == 0:
-            pl.when(is_mid == 1)(send_rest)
+            pl.when(is_outer == 1)(send_rest)
 
         def forward(q, carry, half=half):
             x = pair_of_blocks(prod_in, half, 2 * q)
@@ -477,13 +485,20 @@
         lax.fori_loop(0, n_blocks // 2, inverse, 0)
         if half < halves - 1:
             send_pair(n_blocks // 2 - 1, half)
+        if half == max(halves - 2, 0):
+            for k in range(1, PLANES):
+                gate_line(k, flip(plane, k, PLANES)).wait_recv()
+            gate_in[spot] = gate_mid[:, spot]
+            for k in range(1, team):
+                gate_copy(k, spot).start()
 
     def finish(owner, half, value):
         cols = lanes(owner, half)
         gate = streams_ref[0, :, cols].astype(jnp.float32)
         mixed_ref[:, cols] = (gate * value.astype(jnp.float32)).astype(jnp.bfloat16)
 
-    over_peers(lambda peer: gate_copy(peer, peer).wait_recv())
+    for k in range(1, team):
+        gate_copy(k, flip(spot, k, team)).wait_recv()
     variant = lax.broadcasted_iota(jnp.int32, (n, LANES), 0)
     place = jnp.zeros((n, LANES), jnp.int32)
     for j in range(n):
@@ -535,28 +550,36 @@
         lane = lax.broadcasted_iota(jnp.int32, (1, 2), 1)
         scores_ref[...] = jnp.where(lane == 0, ref_logit - log_total, alt_logit - ref_logit)
 
+    def land(half, k):
+        level = k // team
+        step = jnp.where(level < 2, level, far_step(level - 2))
+        turn = jnp.where(level == 0, k, team - 1 - lax.rem(k, team))
+        peer = peer_at(step, turn)
+        filt_copy(half, peer, peer).wait_recv()
+        finish(peer, half, filt_in[half, peer])
+
     for half in range(halves):
-        if half == halves - 1:
+        def landed(k, carry, half=half):
+            land(half, k)
+            return carry
+
+        last = half == halves - 1
+        lax.fori_loop(1, n - team if last else n, landed, 0)
+        if last:
             score()
-
-        def landed(step, carry, half=half):
-            peer = partner(n - step)
-            filt_copy(half, peer, peer).wait_recv()
-            finish(peer, half, filt_in[half, peer])
-            return carry
-
-        lax.fori_loop(1, n, landed, 0)
+            lax.fori_loop(n - team, n, landed, 0)
 
     def drain(peer):
         for half in range(halves):
             prod_copy(half, peer, me).wait_send()
             filt_copy(half, peer, me).wait_send()
-        gate_copy(peer, me).wait_send()
 
     over_peers(drain)
     for k in range(1, team):
+        gate_copy(k, spot).wait_send()
         part_copy(k, spot).wait_send()
     for k in range(1, PLANES):
+        gate_line(k, plane).wait_send()
         line_copy(k, plane).wait_send()
 
 
@@ -607,7 +630,8 @@
             pltpu.VMEM((n_blocks, 2 * BLOCK, width), jnp.float32),
             pltpu.VMEM((halves, n_blocks, 2 * BLOCK, width), jnp.float32),
             pltpu.VMEM((n, 1, group), GATE),
-            pltpu.VMEM((n, 1, group), GATE),
+            pltpu.VMEM((PLANES, team, 1, group), GATE),
+            pltpu.VMEM((team, PLANES, 1, group), GATE),
             pltpu.VMEM((team, PLANES, vocab + LANES), jnp.float32),
             pltpu.VMEM((team, PLANES, vocab + LANES), jnp.float32),
             pltpu.VMEM((PLANES, 1, vocab + LANES), jnp.float32),
@@ -615,8 +639,8 @@
             pltpu.VMEM((1, model_width), jnp.float32),
         ]
         + [dma((halves, n))] * 4
-        + [dma((n,))] * 2
-        + [dma((team,))] * 2
+        + [dma((PLANES,))] * 2
+        + [dma((team,))] * 4
         + [dma((PLANES,))] * 2
         + [dma((13,))]
         + [pltpu.SemaphoreType.REGULAR] * 3,

time: 56.3 us -> 55.6 us (0.988)
  no operation moved by 1% of the time
where the time goes in v3:
time: 55.6 us; the launch traced here: 54.8 us
  Pallas kernels  52.9 us (95%)
  between operations  1.93 us (3%)
    pallas_call x1, Pallas kernels, fused_shards(): pl.pallas_call(functools.partial(layer_kernel, cfg), out_shape=(jax.Shape...  51.9 us

profile of v3, /device:TPU:12, one launch (start us, length us, event | category | flops | bytes accessed | tf_op | source)
XLA Modules:
  0.0 54.8 jit_solution(5014398408390973524)
XLA Ops:
  1.9 51.9 %shard_map.122 = (bf16[128,4096]{1,0:T(8,128)(2,1)S(1)}, f32[1,2]{1,0:T(1,128)S(1)}) custom-call(s32[16]{0:T(128)} %off_hbm.1, s32[1]{0:T(128)S(6)} %copy.13.ref_id_ref, s32[1]{0:T(128)S(6)} %copy.14.alt_id_ref, bf16[3,128,4096]{2,1,0:T(8,128)(2,1)} %streams_hbm.1, bf16[256,2048]{1,0:T(8,128)(2,1)} %filter_hbm.1, bf16[4096]{0:T(1024)(128)(2,1)} %gain_hbm.1, ...), custom_call_target="tpu_custom_call" | custom-call | tf_op jit(solution)/shard_map/pallas_call | solution.py:619
  53.8 1.0 %shard_map.123 = (bf16[128,4096]{1,0:T(8,128)(2,1)}, f32[1,2]{1,0:T(1,128)}) custom-call(bf16[128,4096]{1,0:T(8,128)(2,1)S(1)} %get-tuple-element.6.mixed_ref, f32[1,2]{1,0:T(1,128)S(1)} %get-tuple-element.7.scores_ref), custom_call_target="tpu_custom_call" | custom-call | tf_op jit(solution)/shard_map/pallas_call | solution.py:651

commit v4 on v3

--- a/solution.py
+++ b/solution.py
@@ -529,7 +529,12 @@
     line_in[plane] = line_out[plane]
     for k in reversed(range(1, PLANES)):
         line_copy(k, plane).start()
-    for k in range(1, n_blocks // 2):
+
+    @pl.when(is_mid == 1)
+    def _():
+        send_pair(1, halves - 1)
+
+    for k in range(2, n_blocks // 2):
         send_pair(k, halves - 1)
 
     def score():
@@ -555,15 +560,28 @@
         step = jnp.where(level < 2, level, far_step(level - 2))
         turn = jnp.where(level == 0, k, team - 1 - lax.rem(k, team))
         peer = peer_at(step, turn)
-        filt_copy(half, peer, peer).wait_recv()
+        known = is_outer * (peer == release) if half == halves - 1 else 0
+
+        @pl.when(known == 0)
+        def _():
+            filt_copy(half, peer, peer).wait_recv()
+
         finish(peer, half, filt_in[half, peer])
 
+    release = peer_at(2, 2)
     for half in range(halves):
         def landed(k, carry, half=half):
             land(half, k)
             return carry
 
         last = half == halves - 1
+        if last:
+
+            @pl.when(is_outer == 1)
+            def _():
+                filt_copy(half, release, release).wait_recv()
+                send_pair(1, half)
+
         lax.fori_loop(1, n - team if last else n, landed, 0)
         if last:
             score()

time: 55.6 us -> 55.1 us (level)
  no operation moved by 1% of the time
where the time goes in v4:
time: 55.1 us; the launch traced here: 54.9 us
  Pallas kernels  53 us (96%)
  between operations  1.93 us (4%)
    pallas_call x1, Pallas kernels, fused_shards(): pl.pallas_call(functools.partial(layer_kernel, cfg), out_shape=(jax.Shape...  51.9 us

profile of v4, /device:TPU:12, one launch (start us, length us, event | category | flops | bytes accessed | tf_op | source)
XLA Modules:
  0.0 54.9 jit_solution(13134325165164072207)
XLA Ops:
  1.9 51.9 %shard_map.122 = (bf16[128,4096]{1,0:T(8,128)(2,1)S(1)}, f32[1,2]{1,0:T(1,128)S(1)}) custom-call(s32[16]{0:T(128)} %off_hbm.1, s32[1]{0:T(128)S(6)} %copy.13.ref_id_ref, s32[1]{0:T(128)S(6)} %copy.14.alt_id_ref, bf16[3,128,4096]{2,1,0:T(8,128)(2,1)} %streams_hbm.1, bf16[256,2048]{1,0:T(8,128)(2,1)} %filter_hbm.1, bf16[4096]{0:T(1024)(128)(2,1)} %gain_hbm.1, ...), custom_call_target="tpu_custom_call" | custom-call | tf_op jit(solution)/shard_map/pallas_call | solution.py:637
  53.9 1.0 %shard_map.123 = (bf16[128,4096]{1,0:T(8,128)(2,1)}, f32[1,2]{1,0:T(1,128)}) custom-call(bf16[128,4096]{1,0:T(8,128)(2,1)S(1)} %get-tuple-element.6.mixed_ref, f32[1,2]{1,0:T(1,128)S(1)} %get-tuple-element.7.scores_ref), custom_call_target="tpu_custom_call" | custom-call | tf_op jit(solution)/shard_map/pallas_call | solution.py:669

commit v5 on v4

--- a/solution.py
+++ b/solution.py
@@ -568,7 +568,15 @@
 
         finish(peer, half, filt_in[half, peer])
 
-    release = peer_at(2, 2)
+    release = peer_at(2, team - 2)
+
+    def sent(half, first, last):
+        def step(k, carry):
+            filt_copy(half, partner(k), me).wait_send()
+            return carry
+
+        lax.fori_loop(first, last, step, 0)
+
     for half in range(halves):
         def landed(k, carry, half=half):
             land(half, k)
@@ -582,23 +590,27 @@
                 filt_copy(half, release, release).wait_recv()
                 send_pair(1, half)
 
+            for early in range(halves):
+                over_peers(lambda peer, early=early: prod_copy(early, peer, me).wait_send())
+            for early in range(halves - 1):
+                sent(early, 1, n)
+            for k in range(1, team):
+                gate_copy(k, spot).wait_send()
+                part_copy(k, spot).wait_send()
+            for k in range(1, PLANES):
+                gate_line(k, plane).wait_send()
+
         lax.fori_loop(1, n - team if last else n, landed, 0)
         if last:
             score()
-            lax.fori_loop(n - team, n, landed, 0)
-
-    def drain(peer):
-        for half in range(halves):
-            prod_copy(half, peer, me).wait_send()
-            filt_copy(half, peer, me).wait_send()
-
-    over_peers(drain)
-    for k in range(1, team):
-        gate_copy(k, spot).wait_send()
-        part_copy(k, spot).wait_send()
-    for k in range(1, PLANES):
-        gate_line(k, plane).wait_send()
-        line_copy(k, plane).wait_send()
+            for k in range(1, PLANES):
+                line_copy(k, plane).wait_send()
+            sent(half, 1, team + 1)
+            sent(half, 2 * team + 1, n)
+            for k in range(n - team, n):
+                land(half, k)
+    for k in range(team + 1, 2 * team + 1):
+        filt_copy(halves - 1, partner(k), me).wait_send()
 
 
 def store_kernel(mixed_ref, scores_ref, mixed_hbm, scores_hbm, sem):

time: 55.1 us -> 54.5 us (0.989)
  Pallas kernels: 53 us -> 52.4 us
where the time goes in v5:
time: 54.5 us; the launch traced here: 54.4 us
  Pallas kernels  52.4 us (96%)
  between operations  1.93 us (4%)
    pallas_call x1, Pallas kernels, fused_shards(): pl.pallas_call(functools.partial(layer_kernel, cfg), out_shape=(jax.Shape...  51.4 us

profile of v5, /device:TPU:12, one launch (start us, length us, event | category | flops | bytes accessed | tf_op | source)
XLA Modules:
  0.0 54.4 jit_solution(6768176525375929554)
XLA Ops:
  1.9 51.4 %shard_map.122 = (bf16[128,4096]{1,0:T(8,128)(2,1)S(1)}, f32[1,2]{1,0:T(1,128)S(1)}) custom-call(s32[16]{0:T(128)} %off_hbm.1, s32[1]{0:T(128)S(6)} %copy.13.ref_id_ref, s32[1]{0:T(128)S(6)} %copy.14.alt_id_ref, bf16[3,128,4096]{2,1,0:T(8,128)(2,1)} %streams_hbm.1, bf16[256,2048]{1,0:T(8,128)(2,1)} %filter_hbm.1, bf16[4096]{0:T(1024)(128)(2,1)} %gain_hbm.1, ...), custom_call_target="tpu_custom_call" | custom-call | tf_op jit(solution)/shard_map/pallas_call | solution.py:649
  53.4 1.0 %shard_map.123 = (bf16[128,4096]{1,0:T(8,128)(2,1)}, f32[1,2]{1,0:T(1,128)}) custom-call(bf16[128,4096]{1,0:T(8,128)(2,1)S(1)} %get-tuple-element.6.mixed_ref, f32[1,2]{1,0:T(1,128)S(1)} %get-tuple-element.7.scores_ref), custom_call_target="tpu_custom_call" | custom-call | tf_op jit(solution)/shard_map/pallas_call | solution.py:681

commit v6 on v5

--- a/solution.py
+++ b/solution.py
@@ -154,7 +154,7 @@
     prod_out, prod_in, filt_out, filt_in, spec, taps,
     gate_out, gate_mid, gate_in, part_out, part_in, line_out, line_in, gain_rows,
     ps_sem, pr_sem, fs_sem, fr_sem, gs_sem, gr_sem, hs_sem, hr_sem, qs_sem, qr_sem, ls_sem, lr_sem, in_sem,
-    side_in, mids_in, far_side_in,
+    side_in, mids_in, far_side_in, across_in,
 ):
     n, halves, rows, width, vocab, model_width = cfg
     me = lax.axis_index("seq")
@@ -189,17 +189,6 @@
     def signal(sem, peer):
         pl.semaphore_signal(sem, inc=1, device_id={"seq": peer}, device_id_type=MESH)
 
-    def greet(plane_step, first):
-        for k in range(first, team):
-            signal(barrier, peer_at(plane_step, k))
-
-    @pl.when(is_mid == 1)
-    def _():
-        greet(3, 0)
-        greet(1, 0)
-
-    greet(0, 1)
-
     def early_step(k):
         mid_steps, outer_steps = (3, 0, 1, 2), (1, 0, 2, 3)
         return outer_steps[k] + (mid_steps[k] - outer_steps[k]) * is_mid
@@ -210,10 +199,35 @@
         part = (pl.ds(1, 2), slice(None), pl.ds(first, share))
         return pltpu.make_async_copy(streams_hbm.at[part], streams_ref.at[part], in_sem.at[k])
 
+    plane_loads = [plane_stream(k) for k in range(PLANES)]
+    plane_loads[0].start()
+    half_team = team // 2
+    side = spot // half_team
+
+    def greet(plane_step, first, last):
+        for k in range(first, last):
+            signal(barrier, peer_at(plane_step, k))
+
+    greet(0, 1, half_team)
+
+    @pl.when(is_mid == 1)
+    def _():
+        greet(3, 0, half_team)
+
+        @pl.when(side == 0)
+        def _():
+            greet(3, half_team, team)
+            greet(0, half_team, team)
+
+        greet(1, 0, team)
+
+    @pl.when(is_outer == 1)
+    def _():
+        greet(0, half_team, team)
+
     def load(src, dst, sem):
         return pltpu.make_async_copy(src, dst, in_sem.at[sem])
 
-    plane_loads = [plane_stream(k) for k in range(PLANES)]
     gate_load = load(streams_hbm.at[0], streams_ref.at[0], 4)
     off_load = load(off_hbm, off_ref, 5)
     tap_loads = [
@@ -227,7 +241,7 @@
         load(gain_hbm, gain_ref, 11),
         load(unembed_hbm, unembed_ref, 12),
     ]
-    for each in plane_loads + [off_load, gate_load] + tap_loads + late_loads:
+    for each in plane_loads[1:] + [off_load, gate_load]:
         each.start()
 
     def lanes(owner, half):
@@ -300,12 +314,12 @@
 
         lax.fori_loop(0, team, step, 0)
 
-    def send_plane(half, plane_step, first):
+    def send_plane(half, plane_step, first, last):
         def step(k, carry):
             prod_copy(half, peer_at(plane_step, k), me).start()
             return carry
 
-        lax.fori_loop(first, team, step, 0)
+        lax.fori_loop(first, last, step, 0)
 
     @pl.when(is_outer == 1)
     def _():
@@ -318,13 +332,27 @@
 
     @pl.when(is_mid == 1)
     def _():
-        pl.semaphore_wait(barrier, 2 * team - 1)
-
-    send_plane(0, early_step(0), 0)
+        pl.semaphore_wait(barrier, team - 1 + side * team)
+
+        @pl.when(side == 1)
+        def _():
+            for k in range(half_team, team):
+                signal(across_in, peer_at(3, k))
+                signal(across_in, peer_at(0, k))
+
+    send_plane(0, early_step(0), 0, half_team)
+
+    @pl.when(is_mid * (1 - side) == 1)
+    def _():
+        pl.semaphore_wait(across_in, team)
+
+    send_plane(0, early_step(0), half_team, team)
+    for each in tap_loads + late_loads:
+        each.start()
     plane_loads[1].wait()
     make_plane(0, 0)
     prod_in[0, me] = prod_out[0, me]
-    send_plane(0, 0, 1)
+    send_plane(0, 0, 1, team)
 
     @pl.when(is_mid == 1)
     def _():
@@ -339,7 +367,7 @@
     def _():
         pl.semaphore_wait(mids_in, 1)
 
-    send_plane(0, early_step(2), 0)
+    send_plane(0, early_step(2), 0, team)
     plane_loads[3].wait()
     make_plane(0, early_step(3))
 
@@ -349,7 +377,7 @@
     def _():
         signal(far_side_in, peer_at(1, 0))
 
-    send_plane(0, early_step(3), 0)
+    send_plane(0, early_step(3), 0, team)
     for half in range(1, halves):
         for k in range(PLANES):
             make_plane(half, k)
@@ -673,7 +701,7 @@
         + [dma((team,))] * 4
         + [dma((PLANES,))] * 2
         + [dma((13,))]
-        + [pltpu.SemaphoreType.REGULAR] * 3,
+        + [pltpu.SemaphoreType.REGULAR] * 4,
         compiler_params=pltpu.CompilerParams(
             collective_id=0, has_side_effects=True, vmem_limit_bytes=48 * 2**20
         ),

time: 54.5 us -> 54.6 us (level)
  no operation moved by 1% of the time
where the time goes in v6:
time: 54.6 us; the launch traced here: 54.4 us
  Pallas kernels  52.5 us (96%)
  between operations  1.93 us (4%)
    pallas_call x1, Pallas kernels, fused_shards(): pl.pallas_call(functools.partial(layer_kernel, cfg), out_shape=(jax.Shape...  51.5 us

profile of v6, /device:TPU:12, one launch (start us, length us, event | category | flops | bytes accessed | tf_op | source)
XLA Modules:
  0.0 54.4 jit_solution(4580115028895220482)
XLA Ops:
  1.9 51.5 %shard_map.122 = (bf16[128,4096]{1,0:T(8,128)(2,1)S(1)}, f32[1,2]{1,0:T(1,128)S(1)}) custom-call(s32[16]{0:T(128)} %off_hbm.1, s32[1]{0:T(128)S(6)} %copy.13.ref_id_ref, s32[1]{0:T(128)S(6)} %copy.14.alt_id_ref, bf16[3,128,4096]{2,1,0:T(8,128)(2,1)} %streams_hbm.1, bf16[256,2048]{1,0:T(8,128)(2,1)} %filter_hbm.1, bf16[4096]{0:T(1024)(128)(2,1)} %gain_hbm.1, ...), custom_call_target="tpu_custom_call" | custom-call | tf_op jit(solution)/shard_map/pallas_call | solution.py:677
  53.4 1.0 %shard_map.123 = (bf16[128,4096]{1,0:T(8,128)(2,1)}, f32[1,2]{1,0:T(1,128)}) custom-call(bf16[128,4096]{1,0:T(8,128)(2,1)S(1)} %get-tuple-element.6.mixed_ref, f32[1,2]{1,0:T(1,128)S(1)} %get-tuple-element.7.scores_ref), custom_call_target="tpu_custom_call" | custom-call | tf_op jit(solution)/shard_map/pallas_call | solution.py:709
